TPU v7x, 256 devices: a whole 4x4x8 slice. The times are simulated.
256 devices in a mesh: space: 16 (over x, z_hi), tm: 16 (over y, z_lo, core).
Axes of the slice: x: 4, y: 4, z: 8 (z_hi: 4, z_lo: 2; z = z_hi * 2 + z_lo), core: 2. Of those that a mesh axis runs over, the one named last changes fastest.
Arguments:
- latent: float32 [24, 1024, 2048], P(None, 'space', 'tm'), may hold values from -1.8 to 1.8
- events: int32 [24, 1024, 2048], P(None, 'space', 'tm'), may hold values from 0 to 7
- log_base: float32 [24, 1024, 2048], P(None, 'space', 'tm'), may hold values from -1.5 to 0.5
- innovation: float32 [24, 1024, 2048], P(None, 'space', 'tm'), may hold values from -6 to 6
- kappa_sq: float32 [24, 1024], replicated, may hold values from 0.3 to 3
- chol_factor: float32 [2048, 2048], P(None, 'tm'), as said below
- step_size: float32 [1], replicated, may hold values from 0.02 to 0.08
Outputs:
- gradient: float32 [24, 1024, 2048], P(None, 'space', 'tm')
- proposal: float32 [24, 1024, 2048], P(None, 'space', 'tm')
Inputs may be any that keep to these rules, and one draw needn't show every extreme that they name: chol_factor is lower triangular with a positive diagonal.
All inputs are finite; a program needn't handle non-finite values.
Results may differ from a plain program's by a relative error of at most 0.000067.
Values sent between devices are 32-bit elements; how exact they have to be, the bound alone decides.
A program may use at most 64 MiB of HBM per device.

v0:
```python
import jax
import jax.numpy as jnp
from jax import lax
from jax.sharding import PartitionSpec as P


def halo(block, width):
    count = lax.axis_size("space")
    forward = [(i, i + 1) for i in range(count - 1)]
    backward = [(target, source) for source, target in forward]
    cols = block.shape[1]
    low = lax.ppermute(lax.slice_in_dim(block, cols - width, None, axis=1), "space", forward)
    high = lax.ppermute(lax.slice_in_dim(block, 0, width, axis=1), "space", backward)
    return jnp.concatenate([low, block, high], axis=1)


def operate(extended, kappa_cols):
    centre = extended[:, 1:-1]
    row_padded = jnp.pad(centre, ((1, 1), (0, 0), (0, 0)))
    beside = row_padded[2:] + row_padded[:-2]
    beside = beside + extended[:, 2:] + extended[:, :-2]
    return (kappa_cols[:, :, None] + 4.0) * centre - beside


def gather_factor(chol_cols):
    n = lax.axis_size("tm")
    T, B = chol_cols.shape
    H = (n + 1) * B // 2
    tail = T - H
    j = lax.axis_index("tm")
    pairs = [(i, n - 1 - i) for i in range(n // 2)]
    sent = lax.ppermute(chol_cols[T - tail :], "tm", pairs)
    own_low = lax.dynamic_slice_in_dim(chol_cols, j * B, H, axis=0)
    partner = n - 1 - j
    length = (n - partner) * B - H
    shifted = lax.dynamic_slice_in_dim(
        jnp.concatenate([sent, jnp.zeros((H, B), sent.dtype)], axis=0), tail - length, H, axis=0
    )
    own_tail = chol_cols[T - H :]
    rows = lax.broadcasted_iota(jnp.int32, (H, B), 0)
    own_high = jnp.where(rows < length, shifted, own_tail)
    piece = jnp.where(j < n // 2, own_low, own_high)
    gathered = lax.all_gather(piece, "tm", axis=0, tiled=False)
    blocks = []
    for c in range(n):
        if c < n // 2:
            p = n - 1 - c
            length_c = (n - c) * B - H
            nonzero = jnp.concatenate([gathered[c], gathered[p, :length_c]], axis=0)
        else:
            p = n - 1 - c
            length_p = (n - p) * B - H
            nonzero = gathered[c, length_p:]
        blocks.append(jnp.concatenate([jnp.zeros((c * B, B), nonzero.dtype), nonzero], axis=0))
    return jnp.concatenate(blocks, axis=1)


def local(latent, events, log_base, innovation, kappa_sq, chol_factor, step_size):
    row_count, col_count, time_count = latent.shape
    space_count = lax.axis_size("space")
    col_index = lax.axis_index("space")
    padded_kappa = jnp.pad(kappa_sq, ((0, 0), (1, 1)))
    kappa_wide = lax.dynamic_slice(
        padded_kappa, (jnp.int32(0), col_index * col_count), (row_count, col_count + 2)
    )
    full = gather_factor(chol_factor)
    extended = halo(latent, 2)
    first_pass = operate(extended, kappa_wide)
    cols = lax.broadcasted_iota(jnp.int32, (1, col_count + 2, 1), 1)
    outside = (cols == 0) & (col_index == 0) | (cols == col_count + 1) & (
        col_index == space_count - 1
    )
    first_pass = jnp.where(outside, 0.0, first_pass)
    spatial = operate(first_pass, kappa_wide[:, 1:-1])
    cell_count = row_count * col_count
    flattened = spatial.reshape(cell_count, time_count)
    by_cell = lax.all_to_all(flattened, "tm", 0, 1, tiled=True)
    projected = jnp.dot(
        by_cell, full, precision=lax.Precision.HIGHEST, preferred_element_type=jnp.float32
    )
    prior_cells = lax.dot_general(
        projected,
        full,
        (((1,), (1,)), ((), ())),
        precision=lax.Precision.HIGHEST,
        preferred_element_type=jnp.float32,
    )
    prior = lax.all_to_all(prior_cells, "tm", 1, 0, tiled=True)
    prior_term = prior.reshape(row_count, col_count, time_count)
    gradient = events.astype(jnp.float32) - jnp.exp(log_base + latent) - prior_term
    proposal = latent + step_size[0] * gradient + jnp.sqrt(2.0 * step_size[0]) * innovation
    return (gradient, proposal)


def solution(mesh):
    in_specs = (
        P(None, "space", "tm"),
        P(None, "space", "tm"),
        P(None, "space", "tm"),
        P(None, "space", "tm"),
        P(),
        P(None, "tm"),
        P(),
    )
    out_specs = (P(None, "space", "tm"), P(None, "space", "tm"))
    return jax.shard_map(local, mesh=mesh, in_specs=in_specs, out_specs=out_specs, check_vma=False)
```

profile of v0, /device:TPU:1, one launch (start us, length us, event | category | flops | bytes accessed | tf_op | source)
XLA Modules:
  0.0 197.4 jit_solution(2388541145353253370)
XLA Ops:
  7.2 1.1 slice.126
  8.3 7.4 %collective-permute-start.2 = (f32[960,128]{1,0:T(8,128)S(1)}, f32[960,128]{1,0:T(8,128)S(1)}, u32[]{:S(2)}, u32[]{:S(2)}) collective-permute-start(f32[960,128]{1,0:T(8,128)S(1)} %slice.126), channel_id=1, source_target_pairs={{0,15},{1,14},{2,13},{3,12},{4,11},{5,10},{6,9},{7,8},{16,31},{17,... | collective-permute-start | bytes 1474568 | tf_op jit(solution)/shard_map/ppermute | solution.py:32
  15.7 11.0 %collective-permute-done.2 = f32[960,128]{1,0:T(8,128)S(1)} collective-permute-done((f32[960,128]{1,0:T(8,128)S(1)}, f32[960,128]{1,0:T(8,128)S(1)}, u32[]{:S(2)}, u32[]{:S(2)}) %collective-permute-start.2) | collective-permute-done | bytes 491552 | tf_op jit(solution)/shard_map/ppermute | solution.py:32
  26.7 2.3 %fusion.13 = f32[1088,128]{1,0:T(8,128)} fusion(s32[]{:T(128)S(6)} %select_n.29, f32[960,128]{1,0:T(8,128)S(1)} %collective-permute-done.2, f32[2048,128]{1,0:T(8,128)} %param.12, s32[]{:T(128)S(6)} %select_n.28, pred[1088]{0:T(1024)(128)(4,1)S(1)} %iota_compare_fusion, pred[]{:T(512)S(6)} %lt.20), kind=kLoop, calls=%fused_computation.40 | loop fusion | flops 278528 | bytes 2163785 | tf_op jit(solution)/shard_map/jit(_where)/select_n | solution.py:42
  29.0 1.0 fusion.17
  29.9 4.9 %collective-permute-start = (f32[24,2,128]{2,1,0:T(2,128)S(1)}, f32[24,2,128]{2,1,0:T(2,128)S(1)}, u32[]{:S(2)}, u32[]{:S(2)}) collective-permute-start(f32[24,2,128]{2,1,0:T(2,128)S(1)} %get-tuple-element.12), channel_id=1, source_target_pairs={{0,16},{16,32},{32,48},{48,64},{64,80},{80,96},{96,112},{112,128},... | collective-permute-start | bytes 73736 | tf_op jit(solution)/shard_map/ppermute | solution.py:12
  34.8 1.3 collective-permute-start.1
  38.0 3.3 %collective-permute-done.1 = f32[24,2,128]{2,1,0:T(2,128)S(1)} collective-permute-done((f32[24,2,128]{2,1,0:T(2,128)S(1)}, f32[24,2,128]{2,1,0:T(2,128)S(1)}, u32[]{:S(2)}, u32[]{:S(2)}) %collective-permute-start.1) | collective-permute-done | bytes 24608 | tf_op jit(solution)/shard_map/ppermute | solution.py:13
  41.3 1.2 pad_maximum_fusion
  42.5 1.7 fusion.4
  44.3 1.2 fusion.8
  45.5 7.7 %all-to-all-start = ((f32[16,96,128]{2,1,0:T(8,128)}), f32[16,96,128]{2,1,0:T(8,128)S(1)}, u32[]{:S(2)}, u32[]{:S(2)}) async-start(f32[16,96,128]{2,1,0:T(8,128)} %bitcast), calls=%async_computation | async-start | bytes 1572864 | tf_op jit(solution)/shard_map/all_to_all | solution.py:77
  53.2 44.7 %all-gather.3.cloned.1.call-done = f32[17408,128]{1,0:T(8,128)} async-done(((f32[1088,128]{1,0:T(8,128)}), f32[17408,128]{1,0:T(8,128)}) %all-gather.3.cloned.1.call-update) | async-done | bytes 8912912 | tf_op jit(solution)/shard_map/all_gather | solution.py:43
  100.5 0.9 slice_bitcast_fusion.11
  101.4 0.9 slice_bitcast_fusion.10
  102.4 1.0 slice_bitcast_fusion.9
  103.4 1.0 slice_bitcast_fusion.8
  104.3 1.0 slice_bitcast_fusion.7
  105.3 1.0 slice_bitcast_fusion.6
  106.3 1.0 slice_bitcast_fusion.5
  107.3 1.0 slice_bitcast_fusion.4
  108.3 1.0 slice_bitcast_fusion.3
  109.4 1.1 slice_bitcast_fusion.2
  110.4 1.1 slice_bitcast_fusion.1
  111.5 1.1 slice_bitcast_fusion
  112.6 2.6 %fusion.16 = (f32[1088,128]{1,0:T(8,128)S(1)}, f32[1088,128]{1,0:T(8,128)S(1)}, f32[1088,128]{1,0:T(8,128)S(1)}, f32[1088,128]{1,0:T(8,128)S(1)}, f32[1088,128]{...) fusion(f32[17408,128]{1,0:T(8,128)} %all-gather.3.cloned.1.call-done), kind=kLoop, calls=%fused_computation.63 | loop fusion | bytes 8912896 | tf_op jit(solution)/shard_map/slice | solution.py:49
  115.1 1.1 maximum_dynamic-update-slice_fusion.7
  116.2 1.4 maximum_dynamic-update-slice_fusion.6
  117.6 1.4 maximum_dynamic-update-slice_fusion.5
  119.0 1.4 maximum_dynamic-update-slice_fusion.4
  120.4 1.4 maximum_dynamic-update-slice_fusion.3
  121.8 1.3 maximum_dynamic-update-slice_fusion.2
  123.1 1.3 maximum_dynamic-update-slice_fusion.1
  124.4 1.4 maximum_dynamic-update-slice_fusion
  125.8 1.1 pad_dynamic-update-slice_fusion.7
  126.9 1.1 pad_dynamic-update-slice_fusion.6
  128.0 1.1 pad_dynamic-update-slice_fusion.5
  130.0 1.1 pad_dynamic-update-slice_fusion.4
  131.0 1.1 pad_dynamic-update-slice_fusion.3
  132.1 1.1 pad_dynamic-update-slice_fusion.2
  133.2 1.1 pad_dynamic-update-slice_fusion.1
  134.3 1.1 pad_dynamic-update-slice_fusion
  135.4 13.5 %fusion.9 = f32[96,2048]{1,0:T(8,128)S(1)} fusion(f32[2048,2048]{1,0:T(8,128)} %pad_dynamic-update-slice_fusion, f32[16,96,128]{2,1,0:T(8,128)S(1)} %all-to-all-done), kind=kOutput, calls=%fused_computation.33 | convolution fusion | flops 4831838208 | bytes 18350080 | tf_op jit(solution)/shard_map/dot_general | solution.py:78
  148.9 19.8 %convolution_bitcast_fusion = f32[12,16,8,128]{3,2,1,0:T(8,128)S(1)} fusion(f32[96,2048]{1,0:T(8,128)S(1)} %fusion.9, f32[2048,2048]{1,0:T(8,128)} %pad_dynamic-update-slice_fusion), kind=kOutput, calls=%fused_computation | convolution fusion | flops 4831838208 | bytes 18350080 | tf_op jit(solution)/shard_map/dot_general | solution.py:81
  168.7 1.0 copy.21
  169.7 5.2 %all-to-all-start.1 = ((f32[96,16,128]{2,0,1:T(8,128)}), f32[96,16,128]{2,0,1:T(8,128)S(1)}, u32[]{:S(2)}, u32[]{:S(2)}) async-start(f32[96,16,128]{2,0,1:T(8,128)} %bitcast.53), calls=%async_computation.1 | async-start | bytes 1572864 | tf_op jit(solution)/shard_map/all_to_all | solution.py:88
  175.6 12.3 %all-to-all-done.1 = f32[96,16,128]{2,0,1:T(8,128)S(1)} async-done(((f32[96,16,128]{2,0,1:T(8,128)}), f32[96,16,128]{2,0,1:T(8,128)S(1)}, u32[]{:S(2)}, u32[]{:S(2)}) %all-to-all-start.1) | async-done | bytes 786464 | tf_op jit(solution)/shard_map/all_to_all | solution.py:88
  187.9 2.7 %multiply_add_fusion = (f32[24,64,128]{2,1,0:T(8,128)}, f32[24,64,128]{2,1,0:T(8,128)}) fusion(f32[24,64,128]{2,1,0:T(8,128)S(1)} %copy-done.1, f32[24,64,128]{2,1,0:T(8,128)S(1)} %copy-done, f32[]{:T(128)S(6)} %sqrt.3, f32[]{:T(128)} %bitcast.54, f32[24,64,128]{2,1,0:T(8,128)S(1)} %bitcast.72, f32[24,64,128]{2,1,0:T(8,128)S(1)} %copy-done.2, ...), kind=kLoop, calls=%fused_computation.37 | loop fusion | flops 1572864 | bytes 5505032 | tf_op jit(solution)/shard_map/add | solution.py:91
  (33 shorter events, 5.3 us)
Async XLA Ops:
  7.2 90.8 %all-gather.3.cloned.1.call-start = ((), (), s32[]{:S(2)}) async-start(), calls=%async_computation.2 | async-start | bytes 9469952 | tf_op jit(solution)/shard_map/all_gather | solution.py:43
  8.3 18.4 %collective-permute-start.2 = (f32[960,128]{1,0:T(8,128)S(1)}, f32[960,128]{1,0:T(8,128)S(1)}, u32[]{:S(2)}, u32[]{:S(2)}) collective-permute-start(f32[960,128]{1,0:T(8,128)S(1)} %slice.126), channel_id=1, source_target_pairs={{0,15},{1,14},{2,13},{3,12},{4,11},{5,10},{6,9},{7,8},{16,31},{17,... | collective-permute-start | bytes 1474568 | tf_op jit(solution)/shard_map/ppermute | solution.py:32
  29.9 8.1 %collective-permute-start = (f32[24,2,128]{2,1,0:T(2,128)S(1)}, f32[24,2,128]{2,1,0:T(2,128)S(1)}, u32[]{:S(2)}, u32[]{:S(2)}) collective-permute-start(f32[24,2,128]{2,1,0:T(2,128)S(1)} %get-tuple-element.12), channel_id=1, source_target_pairs={{0,16},{16,32},{32,48},{48,64},{64,80},{80,96},{96,112},{112,128},... | collective-permute-start | bytes 73736 | tf_op jit(solution)/shard_map/ppermute | solution.py:12
  34.8 6.4 %collective-permute-start.1 = (f32[24,2,128]{2,1,0:T(2,128)S(1)}, f32[24,2,128]{2,1,0:T(2,128)S(1)}, u32[]{:S(2)}, u32[]{:S(2)}) collective-permute-start(f32[24,2,128]{2,1,0:T(2,128)S(1)} %get-tuple-element.13), channel_id=1, source_target_pairs={{16,0},{32,16},{48,32},{64,48},{80,64},{96,80},{112,96},{128,112},... | collective-permute-start | bytes 73736 | tf_op jit(solution)/shard_map/ppermute | solution.py:13
  45.5 89.9 %all-to-all-start = ((f32[16,96,128]{2,1,0:T(8,128)}), f32[16,96,128]{2,1,0:T(8,128)S(1)}, u32[]{:S(2)}, u32[]{:S(2)}) async-start(f32[16,96,128]{2,1,0:T(8,128)} %bitcast), calls=%async_computation | async-start | bytes 1572864 | tf_op jit(solution)/shard_map/all_to_all | solution.py:77
  135.4 52.5 %copy-start = (f32[24,64,128]{2,1,0:T(8,128)S(1)}, f32[24,64,128]{2,1,0:T(8,128)}, u32[]{:S(2)}) copy-start(f32[24,64,128]{2,1,0:T(8,128)} %param.7) | copy-start | bytes 2359300
  135.4 52.5 %copy-start.1 = (f32[24,64,128]{2,1,0:T(8,128)S(1)}, f32[24,64,128]{2,1,0:T(8,128)}, u32[]{:S(2)}) copy-start(f32[24,64,128]{2,1,0:T(8,128)} %param.10) | copy-start | bytes 2359300
  135.4 52.5 %copy-start.2 = (f32[24,64,128]{2,1,0:T(8,128)S(1)}, f32[24,64,128]{2,1,0:T(8,128)}, u32[]{:S(2)}) copy-start(f32[24,64,128]{2,1,0:T(8,128)} %param.9) | copy-start | bytes 2359300
  169.7 18.2 %all-to-all-start.1 = ((f32[96,16,128]{2,0,1:T(8,128)}), f32[96,16,128]{2,0,1:T(8,128)S(1)}, u32[]{:S(2)}, u32[]{:S(2)}) async-start(f32[96,16,128]{2,0,1:T(8,128)} %bitcast.53), calls=%async_computation.1 | async-start | bytes 1572864 | tf_op jit(solution)/shard_map/all_to_all | solution.py:88
Sparse Core Ops, SparseCore 0:
  29.1 68.8 all-gather.2
where the time goes:
time: 199 us; the launch traced here: 197 us
  waiting for transfers between devices  71.3 us (36%)
  matrix products  33.3 us (17%)
  local copies, waits for them, and re-layouts  29.8 us (15%)
  starting transfers between devices  26.5 us (13%)
  other arithmetic  21.5 us (11%)
  between operations  15 us (8%)
    all_gather x1, waiting for transfers between devices, gather_factor(): gathered = lax.all_gather(piece, 'tm', axis=0, tiled=False)  44.7 us
    dot_general x1, matrix products, local(): lax.dot_general(projected, full, (((1,), (1,)), ((), ())), precision=lax....  19.8 us
    dot_general x1, matrix products, local(): jnp.dot(by_cell, full, precision=lax.Precision.HIGHEST, preferred_element...  13.5 us
    all_to_all x1, waiting for transfers between devices, local(): prior = lax.all_to_all(prior_cells, 'tm', 1, 0, tiled=True)  12.3 us
    ppermute x1, waiting for transfers between devices, gather_factor(): sent = lax.ppermute(chol_cols[T - tail:], 'tm', pairs)  11 us
    unnamed x8, other arithmetic  10.7 us
    squeeze x8, local copies, waits for them, and re-layouts, gather_factor(): nonzero = gathered[c, length_p:]  7.81 us
    all_to_all x1, starting transfers between devices, local(): by_cell = lax.all_to_all(flattened, 'tm', 0, 1, tiled=True)  7.71 us
  transfers between devices with their start and end apart: 6, of which 4 were waited for; matrix products, arithmetic and copies ran while one was open for 22% of the time, Pallas kernels for 0%

commit v1 on v0

--- a/solution.py
+++ b/solution.py
@@ -74,7 +74,13 @@
     spatial = operate(first_pass, kappa_wide[:, 1:-1])
     cell_count = row_count * col_count
     flattened = spatial.reshape(cell_count, time_count)
-    by_cell = lax.all_to_all(flattened, "tm", 0, 1, tiled=True)
+    produce_fields_now = lambda field_in, dev_axis: jnp.concatenate(
+        lax.all_to_all(
+            jnp.stack(jnp.split(field_in, lax.axis_size(dev_axis), axis=0)), dev_axis, 0, 0
+        ),
+        axis=1,
+    )
+    by_cell = produce_fields_now(flattened, "tm")
     projected = jnp.dot(
         by_cell, full, precision=lax.Precision.HIGHEST, preferred_element_type=jnp.float32
     )

time: 199 us -> 199 us (level)
  local copies, waits for them, and re-layouts: 29.8 us -> 39.8 us
  waiting for transfers between devices: 71.3 us -> 62.1 us
    unnamed x13 -> x28, local copies, waits for them, and re-layouts: 7.64 us -> 17 us
    all_gather x1, waiting for transfers between devices: 44.7 us -> 35.6 us  [gather_factor(): gathered = lax.all_gather(piece, 'tm', axis=0, tiled=False)]
  transfers between devices with their start and end apart: 6 -> 6, of which waited for: 4 -> 4; matrix products, arithmetic and copies ran while one was open for 22% -> 27% of each run, Pallas kernels for 0% -> 0%
where the time goes in v1:
time: 199 us; the launch traced here: 197 us
  waiting for transfers between devices  62.1 us (31%)
  local copies, waits for them, and re-layouts  39.8 us (20%)
  matrix products  33.3 us (17%)
  starting transfers between devices  26.5 us (13%)
  other arithmetic  20.6 us (10%)
  between operations  15 us (8%)
    all_gather x1, waiting for transfers between devices, gather_factor(): gathered = lax.all_gather(piece, 'tm', axis=0, tiled=False)  35.6 us
    dot_general x1, matrix products, local(): lax.dot_general(projected, full, (((1,), (1,)), ((), ())), precision=lax....  19.8 us
    unnamed x28, local copies, waits for them, and re-layouts  17 us
    dot_general x1, matrix products, local(): jnp.dot(by_cell, full, precision=lax.Precision.HIGHEST, preferred_element...  13.5 us
    all_to_all x1, waiting for transfers between devices, local(): prior = lax.all_to_all(prior_cells, 'tm', 1, 0, tiled=True)  12.3 us
    ppermute x1, waiting for transfers between devices, gather_factor(): sent = lax.ppermute(chol_cols[T - tail:], 'tm', pairs)  11 us
    unnamed x8, other arithmetic  10.7 us
    squeeze x8, local copies, waits for them, and re-layouts, gather_factor(): nonzero = gathered[c, length_p:]  7.81 us
  transfers between devices with their start and end apart: 6, of which 4 were waited for; matrix products, arithmetic and copies ran while one was open for 27% of the time, Pallas kernels for 0%

profile of v1, /device:TPU:1, one launch (start us, length us, event | category | flops | bytes accessed | tf_op | source)
XLA Modules:
  0.0 197.4 jit_solution(6876970166297685279)
XLA Ops:
  7.2 1.1 slice.126
  8.3 7.4 %collective-permute-start.2 = (f32[960,128]{1,0:T(8,128)S(1)}, f32[960,128]{1,0:T(8,128)S(1)}, u32[]{:S(2)}, u32[]{:S(2)}) collective-permute-start(f32[960,128]{1,0:T(8,128)S(1)} %slice.126), channel_id=1, source_target_pairs={{0,15},{1,14},{2,13},{3,12},{4,11},{5,10},{6,9},{7,8},{16,31},{17,... | collective-permute-start | bytes 1474568 | tf_op jit(solution)/shard_map/ppermute | solution.py:32
  15.7 11.0 %collective-permute-done.2 = f32[960,128]{1,0:T(8,128)S(1)} collective-permute-done((f32[960,128]{1,0:T(8,128)S(1)}, f32[960,128]{1,0:T(8,128)S(1)}, u32[]{:S(2)}, u32[]{:S(2)}) %collective-permute-start.2) | collective-permute-done | bytes 491552 | tf_op jit(solution)/shard_map/ppermute | solution.py:32
  26.7 2.3 %fusion.13 = f32[1088,128]{1,0:T(8,128)} fusion(s32[]{:T(128)S(6)} %select_n.29, f32[960,128]{1,0:T(8,128)S(1)} %collective-permute-done.2, f32[2048,128]{1,0:T(8,128)} %param.12, s32[]{:T(128)S(6)} %select_n.28, pred[1088]{0:T(1024)(128)(4,1)S(1)} %iota_compare_fusion, pred[]{:T(512)S(6)} %lt.20), kind=kLoop, calls=%fused_computation.40 | loop fusion | flops 278528 | bytes 2163785 | tf_op jit(solution)/shard_map/jit(_where)/select_n | solution.py:42
  29.0 1.0 fusion.17
  29.9 4.9 %collective-permute-start = (f32[24,2,128]{2,1,0:T(2,128)S(1)}, f32[24,2,128]{2,1,0:T(2,128)S(1)}, u32[]{:S(2)}, u32[]{:S(2)}) collective-permute-start(f32[24,2,128]{2,1,0:T(2,128)S(1)} %get-tuple-element.12), channel_id=1, source_target_pairs={{0,16},{16,32},{32,48},{48,64},{64,80},{80,96},{96,112},{112,128},... | collective-permute-start | bytes 73736 | tf_op jit(solution)/shard_map/ppermute | solution.py:12
  34.8 1.3 collective-permute-start.1
  38.0 3.3 %collective-permute-done.1 = f32[24,2,128]{2,1,0:T(2,128)S(1)} collective-permute-done((f32[24,2,128]{2,1,0:T(2,128)S(1)}, f32[24,2,128]{2,1,0:T(2,128)S(1)}, u32[]{:S(2)}, u32[]{:S(2)}) %collective-permute-start.1) | collective-permute-done | bytes 24608 | tf_op jit(solution)/shard_map/ppermute | solution.py:13
  41.3 1.2 pad_maximum_fusion
  42.5 1.7 fusion.4
  54.6 7.7 %all-to-all-start = ((f32[16,96,128]{2,1,0:T(8,128)}), f32[16,96,128]{2,1,0:T(8,128)S(1)}, u32[]{:S(2)}, u32[]{:S(2)}) async-start(f32[16,96,128]{2,1,0:T(8,128)} %constant_dynamic-update-slice_fusion), calls=%async_computation | async-start | bytes 1572864 | tf_op jit(solution)/shard_map/all_to_all | solution.py:78
  62.3 35.6 %all-gather.3.cloned.1.call-done = f32[17408,128]{1,0:T(8,128)} async-done(((f32[1088,128]{1,0:T(8,128)}), f32[17408,128]{1,0:T(8,128)}) %all-gather.3.cloned.1.call-update) | async-done | bytes 8912912 | tf_op jit(solution)/shard_map/all_gather | solution.py:43
  99.6 0.9 slice_bitcast_fusion.12
  100.5 0.9 slice_bitcast_fusion.11
  101.4 0.9 slice_bitcast_fusion.10
  102.4 1.0 slice_bitcast_fusion.9
  103.4 1.0 slice_bitcast_fusion.8
  104.3 1.0 slice_bitcast_fusion.7
  105.3 1.0 slice_bitcast_fusion.6
  106.3 1.0 slice_bitcast_fusion.5
  107.3 1.0 slice_bitcast_fusion.4
  108.3 1.0 slice_bitcast_fusion.3
  109.4 1.1 slice_bitcast_fusion.2
  110.4 1.1 slice_bitcast_fusion.1
  111.5 1.1 slice_bitcast_fusion
  112.6 2.6 %fusion.16 = (f32[1088,128]{1,0:T(8,128)S(1)}, f32[1088,128]{1,0:T(8,128)S(1)}, f32[1088,128]{1,0:T(8,128)S(1)}, f32[1088,128]{1,0:T(8,128)S(1)}, f32[1088,128]{...) fusion(f32[17408,128]{1,0:T(8,128)} %all-gather.3.cloned.1.call-done), kind=kLoop, calls=%fused_computation.95 | loop fusion | bytes 8912896 | tf_op jit(solution)/shard_map/slice | solution.py:49
  115.1 1.1 maximum_dynamic-update-slice_fusion.7
  116.2 1.4 maximum_dynamic-update-slice_fusion.6
  117.6 1.4 maximum_dynamic-update-slice_fusion.5
  119.0 1.4 maximum_dynamic-update-slice_fusion.4
  120.4 1.4 maximum_dynamic-update-slice_fusion.3
  121.8 1.3 maximum_dynamic-update-slice_fusion.2
  123.1 1.3 maximum_dynamic-update-slice_fusion.1
  124.4 1.4 maximum_dynamic-update-slice_fusion
  125.8 1.1 pad_dynamic-update-slice_fusion.7
  126.9 1.1 pad_dynamic-update-slice_fusion.6
  128.0 1.1 pad_dynamic-update-slice_fusion.5
  130.0 1.1 pad_dynamic-update-slice_fusion.4
  131.0 1.1 pad_dynamic-update-slice_fusion.3
  132.1 1.1 pad_dynamic-update-slice_fusion.2
  133.2 1.1 pad_dynamic-update-slice_fusion.1
  134.3 1.1 pad_dynamic-update-slice_fusion
  135.4 13.5 %fusion.9 = f32[96,2048]{1,0:T(8,128)S(1)} fusion(f32[2048,2048]{1,0:T(8,128)} %pad_dynamic-update-slice_fusion, f32[16,96,128]{2,1,0:T(8,128)S(1)} %all-to-all-done), kind=kOutput, calls=%fused_computation.33 | convolution fusion | flops 4831838208 | bytes 18350080 | tf_op jit(solution)/shard_map/dot_general | solution.py:84
  148.9 19.8 %convolution_bitcast_fusion = f32[12,16,8,128]{3,2,1,0:T(8,128)S(1)} fusion(f32[96,2048]{1,0:T(8,128)S(1)} %fusion.9, f32[2048,2048]{1,0:T(8,128)} %pad_dynamic-update-slice_fusion), kind=kOutput, calls=%fused_computation | convolution fusion | flops 4831838208 | bytes 18350080 | tf_op jit(solution)/shard_map/dot_general | solution.py:87
  168.7 1.0 copy.35
  169.7 5.2 %all-to-all-start.1 = ((f32[96,16,128]{2,0,1:T(8,128)}), f32[96,16,128]{2,0,1:T(8,128)S(1)}, u32[]{:S(2)}, u32[]{:S(2)}) async-start(f32[96,16,128]{2,0,1:T(8,128)} %bitcast.117), calls=%async_computation.1 | async-start | bytes 1572864 | tf_op jit(solution)/shard_map/all_to_all | solution.py:94
  175.6 12.3 %all-to-all-done.1 = f32[96,16,128]{2,0,1:T(8,128)S(1)} async-done(((f32[96,16,128]{2,0,1:T(8,128)}), f32[96,16,128]{2,0,1:T(8,128)S(1)}, u32[]{:S(2)}, u32[]{:S(2)}) %all-to-all-start.1) | async-done | bytes 786464 | tf_op jit(solution)/shard_map/all_to_all | solution.py:94
  187.9 2.7 %multiply_add_fusion = (f32[24,64,128]{2,1,0:T(8,128)}, f32[24,64,128]{2,1,0:T(8,128)}) fusion(f32[24,64,128]{2,1,0:T(8,128)S(1)} %copy-done.1, f32[24,64,128]{2,1,0:T(8,128)S(1)} %copy-done, f32[]{:T(128)S(6)} %sqrt.3, f32[]{:T(128)} %bitcast.118, f32[24,64,128]{2,1,0:T(8,128)S(1)} %bitcast.152, f32[24,64,128]{2,1,0:T(8,128)S(1)} %copy-done.2, ...), kind=kLoop, calls=%fused_computation.37 | loop fusion | flops 1572864 | bytes 5505032 | tf_op jit(solution)/shard_map/add | solution.py:97
  (49 shorter events, 14.7 us)
Async XLA Ops:
  7.2 90.8 %all-gather.3.cloned.1.call-start = ((), (), s32[]{:S(2)}) async-start(), calls=%async_computation.2 | async-start | bytes 9469952 | tf_op jit(solution)/shard_map/all_gather | solution.py:43
  8.3 18.4 %collective-permute-start.2 = (f32[960,128]{1,0:T(8,128)S(1)}, f32[960,128]{1,0:T(8,128)S(1)}, u32[]{:S(2)}, u32[]{:S(2)}) collective-permute-start(f32[960,128]{1,0:T(8,128)S(1)} %slice.126), channel_id=1, source_target_pairs={{0,15},{1,14},{2,13},{3,12},{4,11},{5,10},{6,9},{7,8},{16,31},{17,... | collective-permute-start | bytes 1474568 | tf_op jit(solution)/shard_map/ppermute | solution.py:32
  29.9 8.1 %collective-permute-start = (f32[24,2,128]{2,1,0:T(2,128)S(1)}, f32[24,2,128]{2,1,0:T(2,128)S(1)}, u32[]{:S(2)}, u32[]{:S(2)}) collective-permute-start(f32[24,2,128]{2,1,0:T(2,128)S(1)} %get-tuple-element.12), channel_id=1, source_target_pairs={{0,16},{16,32},{32,48},{48,64},{64,80},{80,96},{96,112},{112,128},... | collective-permute-start | bytes 73736 | tf_op jit(solution)/shard_map/ppermute | solution.py:12
  34.8 6.4 %collective-permute-start.1 = (f32[24,2,128]{2,1,0:T(2,128)S(1)}, f32[24,2,128]{2,1,0:T(2,128)S(1)}, u32[]{:S(2)}, u32[]{:S(2)}) collective-permute-start(f32[24,2,128]{2,1,0:T(2,128)S(1)} %get-tuple-element.13), channel_id=1, source_target_pairs={{16,0},{32,16},{48,32},{64,48},{80,64},{96,80},{112,96},{128,112},... | collective-permute-start | bytes 73736 | tf_op jit(solution)/shard_map/ppermute | solution.py:13
  54.6 80.8 %all-to-all-start = ((f32[16,96,128]{2,1,0:T(8,128)}), f32[16,96,128]{2,1,0:T(8,128)S(1)}, u32[]{:S(2)}, u32[]{:S(2)}) async-start(f32[16,96,128]{2,1,0:T(8,128)} %constant_dynamic-update-slice_fusion), calls=%async_computation | async-start | bytes 1572864 | tf_op jit(solution)/shard_map/all_to_all | solution.py:78
  135.4 52.5 %copy-start = (f32[24,64,128]{2,1,0:T(8,128)S(1)}, f32[24,64,128]{2,1,0:T(8,128)}, u32[]{:S(2)}) copy-start(f32[24,64,128]{2,1,0:T(8,128)} %param.7) | copy-start | bytes 2359300
  135.4 52.5 %copy-start.1 = (f32[24,64,128]{2,1,0:T(8,128)S(1)}, f32[24,64,128]{2,1,0:T(8,128)}, u32[]{:S(2)}) copy-start(f32[24,64,128]{2,1,0:T(8,128)} %param.10) | copy-start | bytes 2359300
  135.4 52.5 %copy-start.2 = (f32[24,64,128]{2,1,0:T(8,128)S(1)}, f32[24,64,128]{2,1,0:T(8,128)}, u32[]{:S(2)}) copy-start(f32[24,64,128]{2,1,0:T(8,128)} %param.9) | copy-start | bytes 2359300
  169.7 18.2 %all-to-all-start.1 = ((f32[96,16,128]{2,0,1:T(8,128)}), f32[96,16,128]{2,0,1:T(8,128)S(1)}, u32[]{:S(2)}, u32[]{:S(2)}) async-start(f32[96,16,128]{2,0,1:T(8,128)} %bitcast.117), calls=%async_computation.1 | async-start | bytes 1572864 | tf_op jit(solution)/shard_map/all_to_all | solution.py:94
Sparse Core Ops, SparseCore 0:
  29.1 68.8 all-gather.2
